TPU v7x, 32 devices: a whole 2x2x4 slice. The times are simulated.
32 devices in a mesh: feat: 4 (over y, x), label: 8 (over z, core).
Axes of the slice: x: 2, y: 2, z: 4, core: 2. Of those that a mesh axis runs over, the one named last changes fastest.
Arguments:
- documents: bfloat16 [160, 1024], P(None, 'label'), may hold values from -6 to 6
- expand_weight: bfloat16 [1024, 32768], P('label', 'feat'), may hold values from -0.1875 to 0.1875
- sparse_weight: bfloat16 [768, 16, 128, 128], P(('feat', 'label')), may hold values from -0.125 to 0.125
- feature_lists: int32 [768, 16], replicated, may hold values from 0 to 255, as said below
- positives: int32 [160, 8], replicated, may hold values from 0 to 98303
Outputs:
- grad_expand: bfloat16 [1024, 32768], P('label', 'feat')
- grad_sparse: bfloat16 [768, 16, 128, 128], P(('feat', 'label'))
Inputs may be any that keep to these rules, and one draw needn't show every extreme that they name: `feature_lists`: within each aligned group of 24 label blocks (taken in order), the entries name exactly 24 distinct feature blocks from each range of 64 consecutive blocks, each named exactly 4 times in the group; the 16 entries of one label block are distinct.
All inputs are finite; a program needn't handle non-finite values.
Results may differ from a plain program's by a relative error of at most 0.014.
Values may be sent and summed in bfloat16 or wider, within the bound.
No kernel may reach another device: no remote copies, remote signals or barrier semaphores. Data moves between devices by JAX's collectives and lax.ppermute only.
A program may use at most 192 MiB of HBM per device.

v0:
```python
import jax
import jax.numpy as jnp
from jax import lax
from jax.sharding import PartitionSpec as P

BLK = 128
FBLOCKS = 256
SLOTS = 16
LBLK_DEV = 24
CAP = 24


def on_device(documents, expand_weight, sparse_weight, feature_lists, positives):
    feat_count = lax.axis_size("feat")
    label_count = lax.axis_size("label")
    feat_index = lax.axis_index("feat")
    label_index = lax.axis_index("label")
    group = feat_index * label_count + label_index
    doc_count = documents.shape[0]
    width_local = expand_weight.shape[0]
    own_count = expand_weight.shape[1] // BLK
    local_weight = expand_weight.reshape(width_local, own_count, BLK)
    partial_pre = jnp.einsum(
        "dk,kbc->bdc", documents, local_weight, preferred_element_type=jnp.float32
    )
    summed_pre = lax.psum(partial_pre, "label")
    hidden = jnp.maximum(summed_pre, 0.0).astype(jnp.bfloat16)
    mine = lax.dynamic_slice_in_dim(feature_lists, group * LBLK_DEV, LBLK_DEV, 0)

    def sender_list(target):
        rows = lax.dynamic_slice_in_dim(
            feature_lists, (target * label_count + label_index) * LBLK_DEV, LBLK_DEV, 0
        )
        local_ids = feat_index * own_count + jnp.arange(own_count, dtype=jnp.int32)
        used = jnp.any(rows.reshape(-1)[:, None] == local_ids[None, :], axis=0)
        order = jnp.argsort(jnp.where(used, 0, 1).astype(jnp.int32), stable=True)
        return order[:CAP]

    send_index = jax.vmap(sender_list)(jnp.arange(feat_count, dtype=jnp.int32))
    outgoing = jnp.take(hidden, send_index, axis=0)
    incoming = lax.all_to_all(outgoing, "feat", split_axis=0, concat_axis=0, tiled=True)
    present = jnp.any(
        mine.reshape(-1)[:, None] == jnp.arange(FBLOCKS, dtype=jnp.int32)[None, :], axis=0
    )
    ranks = jnp.cumsum(present.reshape(feat_count, own_count).astype(jnp.int32), axis=1) - 1
    position_table = (jnp.arange(feat_count, dtype=jnp.int32)[:, None] * CAP + ranks).reshape(-1)
    slot_position = jnp.take(position_table, mine, axis=0)
    picked = jnp.take(incoming.reshape(feat_count * CAP, doc_count, BLK), slot_position, axis=0)
    logits = jnp.einsum("lsdc,lsce->dle", picked, sparse_weight, preferred_element_type=jnp.float32)
    label_ids = (group * LBLK_DEV + jnp.arange(LBLK_DEV, dtype=jnp.int32))[
        :, None
    ] * BLK + jnp.arange(BLK, dtype=jnp.int32)[None, :]
    targets = jnp.any(positives[:, :, None, None] == label_ids[None, None, :, :], axis=1).astype(
        jnp.float32
    )
    residual = (jax.nn.sigmoid(logits) - targets).astype(jnp.bfloat16)
    grad_sparse = jnp.einsum(
        "lsdc,dle->lsce", picked, residual, preferred_element_type=jnp.float32
    ).astype(jnp.bfloat16)
    back = jnp.einsum("dle,lsce->lsdc", residual, sparse_weight, preferred_element_type=jnp.float32)
    back_rows = back.reshape(LBLK_DEV * SLOTS, doc_count, BLK)
    group_part = jax.ops.segment_sum(
        back_rows, slot_position.reshape(-1), num_segments=feat_count * CAP
    )
    group_part = group_part.astype(jnp.bfloat16).reshape(feat_count, CAP, doc_count, BLK)
    returned = lax.all_to_all(group_part, "feat", split_axis=0, concat_axis=0, tiled=True)
    column_sum = jax.ops.segment_sum(
        returned.astype(jnp.float32).reshape(feat_count * CAP, doc_count, BLK),
        send_index.reshape(-1),
        num_segments=own_count,
    )
    block_grad = lax.psum(column_sum.astype(jnp.bfloat16), "label").astype(jnp.float32)
    grad_hidden = jnp.where(hidden > 0, block_grad, 0.0).astype(jnp.bfloat16)
    grad_expand = jnp.einsum(
        "dk,bdc->kbc", documents, grad_hidden, preferred_element_type=jnp.float32
    )
    grad_expand = grad_expand.reshape(width_local, own_count * BLK).astype(jnp.bfloat16)
    return (grad_expand, grad_sparse)


def solution(mesh):
    return jax.shard_map(
        on_device,
        mesh=mesh,
        in_specs=(
            P(None, "label"),
            P("label", "feat"),
            P(("feat", "label"), None, None, None),
            P(),
            P(),
        ),
        out_specs=(P("label", "feat"), P(("feat", "label"), None, None, None)),
        check_vma=False,
    )
```

profile of v0, /device:TPU:0, one launch (start us, length us, event | category | flops | bytes accessed | tf_op | source)
XLA Modules:
  0.0 502.6 jit_solution(14127657274373574968)
XLA Ops:
  7.2 8.1 %while.1 = (s32[]{:T(128)}, s32[768,16]{0,1:T(8,128)}, s32[4,2]{0,1:T(2,128)S(1)}, s32[4,24,16]{1,2,0:T(8,128)S(1)}, s32[]{:T(128)}) while((s32[]{:T(128)}, s32[768,16]{0,1:T(8,128)}, s32[4,2]{0,1:T(2,128)S(1)}, s32[4,24,16]{1,2,0:T(8,128)S(1)}, s32[]{:T(128)}) %tuple.25), condition=%wide.while_cond, body=%wide.while_body.sunk | while | flops 2 | bytes 9825 | solution.py:31
  7.2 0.1 constant_dynamic-slice_fusion.3
  7.3 0.5 slice.26
  7.8 1.4 bitcast_dynamic-update-slice_fusion.2
  9.3 0.1 constant_dynamic-slice_fusion.3
  9.3 0.5 slice.26
  9.9 1.4 bitcast_dynamic-update-slice_fusion.2
  11.3 0.1 constant_dynamic-slice_fusion.3
  11.4 0.5 slice.26
  11.9 1.4 bitcast_dynamic-update-slice_fusion.2
  13.3 0.1 constant_dynamic-slice_fusion.3
  13.4 0.5 slice.26
  13.9 1.4 bitcast_dynamic-update-slice_fusion.2
  15.4 0.1 copy.20
  15.4 0.1 eq.43
  15.5 0.2 compare_reduce_fusion.1
  15.8 0.1 copy.21
  15.9 1.0 sort.17
  16.9 0.1 copy.25
  17.0 0.1 reshape.170
  17.1 4.0 convolution_bitcast_fusion
  21.1 111.1 %all-reduce.5 = bf16[64,160,128]{2,1,0:T(8,128)(2,1)} all-reduce(f32[64,160,128]{2,1,0:T(8,128)} %convolution_bitcast_fusion), channel_id=1, replica_groups=mesh['feat'=4,'label'=8] {'label'}, use_global_device_ids=true, to_apply=%region_0.0 | all-reduce | flops 1310720 | bytes 7864320 | tf_op jit(solution)/shard_map/psum | solution.py:26
  132.1 3.8 maximum_convert_fusion
  135.9 0.1 copy.24
  136.0 4.8 gather_fusion.1
  140.8 4.5 broadcast_select_fusion.5
  145.3 5.0 all-to-all-start
  150.3 0.8 constant_dynamic-slice_fusion.1
  151.1 0.1 copy.31
  151.2 0.1 eq.47
  151.2 0.1 reshape.162
  151.3 0.1 fusion.16
  151.5 0.1 reshape.157
  151.6 0.2 reduce_window_sum.11
  151.8 0.1 add_add_fusion
  151.9 0.1 add.134
  152.0 2.8 gather_fusion
  154.8 0.1 reshape.161
  154.9 0.1 reshape.186
  155.0 0.1 reshape.178
  155.1 0.1 copy.26
  155.2 0.1 iota_add_fusion
  155.3 3.7 compare_reduce_fusion
  159.0 32.3 %all-to-all-done = bf16[4,24,160,128]{3,2,1,0:T(8,128)(2,1)} async-done(((bf16[4,24,160,128]{3,2,1,0:T(8,128)(2,1)}), bf16[4,24,160,128]{3,2,1,0:T(8,128)(2,1)}, u32[]{:S(2)}, u32[]{:S(2)}) %all-to-all-start) | async-done | bytes 3932192 | tf_op jit(solution)/shard_map/all_to_all | solution.py:41
  191.3 14.7 %gather_fusion.2 = bf16[384,160,128]{2,1,0:T(8,128)(2,1)} fusion(bf16[96,160,128]{2,1,0:T(8,128)(2,1)} %bitcast.3, s32[1024]{0:T(1024)S(1)} %pad_clamp_fusion), kind=kCustom, calls=%fused_computation.2 | custom fusion | bytes 31458816 | tf_op jit(solution)/shard_map/jit(_take)/gather | solution.py:48
  206.0 11.4 %fusion.14 = bf16[160,24,128,1]{2,0,3,1:T(8,128)(2,1)S(1)} fusion(pred[160,24,128]{2,1,0:T(8,128)(4,1)S(1)} %compare_reduce_fusion, bf16[24,16,128,128]{3,2,1,0:T(8,128)(2,1)} %param.7, bf16[24,16,160,128]{3,2,1,0:T(8,128)(2,1)} %bitcast.62, pred[24,16]{1,0:T(8,128)(4,1)S(1)} %get-tuple-element.26), kind=kOutput, calls=%fused_computation.30 | convolution fusion | flops 2024079360 | bytes 29786496 | tf_op jit(solution)/shard_map/lsdc,lsce->dle/dot_general | solution.py:49
  217.4 15.2 %fusion.23 = f32[24,160,16,128]{3,1,2,0:T(8,128)} fusion(bf16[160,24,128,1]{2,0,3,1:T(8,128)(2,1)S(1)} %fusion.14, bf16[24,16,128,128]{3,2,1,0:T(8,128)(2,1)} %param.7), kind=kOutput, calls=%fused_computation.58 | convolution fusion | flops 2013265920 | bytes 45023232 | tf_op jit(solution)/shard_map/dle,lsce->lsdc/dot_general | solution.py:60
  232.6 4.2 broadcast_in_dim.58
  236.8 87.4 %scatter_fusion = f32[96,160,128]{2,1,0:T(8,128)} fusion(f32[96,160,128]{2,1,0:T(8,128)} %broadcast_in_dim.58, s32[384]{0:T(512)S(1)} %reshape.186, f32[384,160,128]{2,1,0:T(8,128)} %bitcast.61), kind=kCustom, calls=%fused_computation.3 | custom fusion | flops 7864320 | bytes 94373376 | tf_op jit(solution)/shard_map/scatter-add | solution.py:62
  324.3 5.8 %convert_element_type.45 = bf16[96,160,128]{2,1,0:T(8,128)(2,1)} convert(f32[96,160,128]{2,1,0:T(8,128)} %scatter_fusion) | non-fusion elementwise | flops 1966080 | bytes 11796480 | tf_op jit(solution)/shard_map/convert_element_type | solution.py:65
  330.1 4.8 all-to-all-start.1
  334.9 0.3 all-reduce.4.cloned.1.call-start
  335.2 0.1 copy.22
  335.3 0.1 reshape.194
  335.4 43.7 %all-to-all-done.1 = bf16[4,24,160,128]{3,2,1,0:T(8,128)(2,1)} async-done(((bf16[4,24,160,128]{3,2,1,0:T(8,128)(2,1)}), bf16[4,24,160,128]{3,2,1,0:T(8,128)(2,1)}, u32[]{:S(2)}, u32[]{:S(2)}) %all-to-all-start.1) | async-done | bytes 3932192 | tf_op jit(solution)/shard_map/all_to_all | solution.py:66
  379.1 6.4 %bitcast_convert_fusion = f32[96,160,128]{2,1,0:T(8,128)} fusion(bf16[4,24,160,128]{3,2,1,0:T(8,128)(2,1)} %all-to-all-done.1), kind=kLoop, calls=%fused_computation.16 | loop fusion | flops 1966080 | bytes 11796480 | tf_op jit(solution)/shard_map/reshape | solution.py:68
  385.5 3.0 broadcast.134
  388.4 22.5 %scatter_fusion.1 = f32[64,160,128]{2,1,0:T(8,128)} fusion(f32[64,160,128]{2,1,0:T(8,128)} %broadcast.134, s32[96]{0:T(128)S(1)} %reshape.194, f32[96,160,128]{2,1,0:T(8,128)} %bitcast_convert_fusion), kind=kCustom, calls=%fused_computation.4 | custom fusion | flops 1966080 | bytes 23593344 | tf_op jit(solution)/shard_map/scatter-add | solution.py:67
  411.0 4.4 convert_element_type.46
  415.3 0.0 all-reduce.4.cloned.1.call-update
  415.4 14.3 %fusion.4 = bf16[24,16,128,128]{3,2,1,0:T(8,128)(2,1)} fusion(bf16[160,24,128,1]{2,0,3,1:T(8,128)(2,1)S(1)} %fusion.14, bf16[24,16,160,128]{3,2,1,0:T(8,128)(2,1)} %bitcast.63, pred[24,16]{1,0:T(8,128)(4,1)S(1)} %get-tuple-element.26), kind=kOutput, calls=%fused_computation.13 | convolution fusion | flops 2027421696 | bytes 29294976 | tf_op jit(solution)/shard_map/lsdc,dle->lsce/dot_general | solution.py:57
  429.6 56.8 %all-reduce.4.cloned.1.call-done = bf16[64,160,128]{2,1,0:T(8,128)(2,1)} async-done(((bf16[64,160,128]{2,1,0:T(8,128)(2,1)}), bf16[64,160,128]{2,1,0:T(8,128)(2,1)}) %all-reduce.4.cloned.1.call-update) | async-done | bytes 2621456 | tf_op jit(solution)/shard_map/psum | solution.py:72
  486.5 5.2 %fusion.13 = bf16[64,128,128]{2,1,0:T(8,128)(2,1)} fusion(bf16[64,160,128]{2,1,0:T(8,128)(2,1)} %all-reduce.4.cloned.1.call-done, bf16[160,128]{1,0:T(8,128)(2,1)S(1)} %copy-done.2, bf16[64,160,128]{2,1,0:T(8,128)(2,1)} %all-reduce.5), kind=kOutput, calls=%fused_computation.29 | convolution fusion | flops 345767936 | bytes 7380992 | tf_op jit(solution)/shard_map/dk,bdc->kbc/dot_general | solution.py:74
  491.6 4.1 copy.28
  (25 shorter events, 0.1 us)
Async XLA Ops:
  7.2 9.9 %copy-start = (bf16[128,8192]{1,0:T(8,128)(2,1)S(1)}, bf16[128,8192]{1,0:T(8,128)(2,1)}, u32[]{:S(2)}) copy-start(bf16[128,8192]{1,0:T(8,128)(2,1)} %param.6) | copy-start | bytes 6291460
  145.3 46.0 %all-to-all-start = ((bf16[4,24,160,128]{3,2,1,0:T(8,128)(2,1)}), bf16[4,24,160,128]{3,2,1,0:T(8,128)(2,1)}, u32[]{:S(2)}, u32[]{:S(2)}) async-start(bf16[4,24,160,128]{3,2,1,0:T(8,128)(2,1)} %broadcast_select_fusion.5), calls=%async_computation | async-start | bytes 7864320 | tf_op jit(solution)/shard_map/all_to_all | solution.py:41
  152.0 3.1 copy-start.3
  330.1 48.9 %all-to-all-start.1 = ((bf16[4,24,160,128]{3,2,1,0:T(8,128)(2,1)}), bf16[4,24,160,128]{3,2,1,0:T(8,128)(2,1)}, u32[]{:S(2)}, u32[]{:S(2)}) async-start(bf16[4,24,160,128]{3,2,1,0:T(8,128)(2,1)} %bitcast.64), calls=%async_computation.1 | async-start | bytes 7864320 | tf_op jit(solution)/shard_map/all_to_all | solution.py:66
  334.9 151.5 %all-reduce.4.cloned.1.call-start = ((), (), s32[]{:S(2)}) async-start(), calls=%async_computation.2 | async-start | bytes 5242880 | tf_op jit(solution)/shard_map/psum | solution.py:72
  415.3 71.1 %copy-start.2 = (bf16[160,128]{1,0:T(8,128)(2,1)S(1)}, bf16[160,128]{1,0:T(8,128)(2,1)}, u32[]{:S(2)}) copy-start(bf16[160,128]{1,0:T(8,128)(2,1)} %param.5) | copy-start | bytes 122884
  415.4 80.4 %copy-start.1 = (bf16[128,8192]{1,0:T(8,128)(2,1)S(1)}, bf16[128,8192]{1,0:T(8,128)(2,1)}, u32[]{:S(2)}) copy-start(bf16[128,8192]{1,0:T(8,128)(2,1)} %param.6) | copy-start | bytes 6291460
Sparse Core Ops, SparseCore 0:
  415.5 70.9 all-reduce.3
where the time goes:
time: 505 us; the launch traced here: 503 us
  other arithmetic  140 us (28%)
  waiting for transfers between devices  133 us (26%)
  blocking collectives  111 us (22%)
  matrix products  50.1 us (10%)
  local copies, waits for them, and re-layouts  44 us (9%)
  between operations  14.2 us (3%)
  starting transfers between devices  10 us (2%)
    psum x1, blocking collectives, on_device(): summed_pre = lax.psum(partial_pre, 'label')  111 us
    scatter-add x1, other arithmetic, on_device(): jax.ops.segment_sum(back_rows, slot_position.reshape(-1), num_segments=fe...  87.4 us
    psum x1, waiting for transfers between devices, on_device(): lax.psum(column_sum.astype(jnp.bfloat16), 'label').astype(jnp.float32)  56.8 us
    all_to_all x1, waiting for transfers between devices, on_device(): lax.all_to_all(group_part, 'feat', split_axis=0, concat_axis=0, tiled=True)  43.7 us
    all_to_all x1, waiting for transfers between devices, on_device(): lax.all_to_all(outgoing, 'feat', split_axis=0, concat_axis=0, tiled=True)  32.3 us
    scatter-add x1, other arithmetic, on_device(): jax.ops.segment_sum(returned.astype(jnp.float32).reshape(feat_count * CAP...  22.5 us
    dot_general x1, matrix products, on_device(): jnp.einsum('dle,lsce->lsdc', residual, sparse_weight, preferred_element_t...  15.2 us
    gather x1, local copies, waits for them, and re-layouts, on_device(): jnp.take(incoming.reshape(feat_count * CAP, doc_count, BLK), slot_positio...  14.7 us
  transfers between devices with their start and end apart: 3, of which 3 were waited for; matrix products, arithmetic and copies ran while one was open for 5% of the time, Pallas kernels for 0%

commit v1 on v0

--- a/solution.py
+++ b/solution.py
@@ -23,7 +23,7 @@
     partial_pre = jnp.einsum(
         "dk,kbc->bdc", documents, local_weight, preferred_element_type=jnp.float32
     )
-    summed_pre = lax.psum(partial_pre, "label")
+    summed_pre = jnp.sum(lax.all_gather(partial_pre, "label"), axis=0)
     hidden = jnp.maximum(summed_pre, 0.0).astype(jnp.bfloat16)
     mine = lax.dynamic_slice_in_dim(feature_lists, group * LBLK_DEV, LBLK_DEV, 0)
 

time: 505 us -> 765 us (1.51)
  waiting for transfers between devices: 133 us -> 485 us
  blocking collectives: 111 us -> 0 us
  other arithmetic: 140 us -> 158 us
    all_gather x0 -> x1, waiting for transfers between devices: none -> 352 us  [on_device(): summed_pre = jnp.sum(lax.all_gather(partial_pre, 'label'), axis=0)]
    psum x1 -> x0, blocking collectives: 111 us -> none  [on_device(): summed_pre = lax.psum(partial_pre, 'label')]
    reduce_sum x0 -> x1, other arithmetic: none -> 18 us  [on_device(): summed_pre = jnp.sum(lax.all_gather(partial_pre, 'label'), axis=0)]
  transfers between devices with their start and end apart: 3 -> 4, of which waited for: 3 -> 4; matrix products, arithmetic and copies ran while one was open for 5% -> 4% of each run, Pallas kernels for 0% -> 0%
where the time goes in v1:
time: 765 us; the launch traced here: 763 us
  waiting for transfers between devices  485 us (63%)
  other arithmetic  158 us (21%)
  matrix products  50.2 us (7%)
  local copies, waits for them, and re-layouts  45 us (6%)
  between operations  14.2 us (2%)
  starting transfers between devices  10.1 us (1%)
    all_gather x1, waiting for transfers between devices, on_device(): summed_pre = jnp.sum(lax.all_gather(partial_pre, 'label'), axis=0)  352 us
    scatter-add x1, other arithmetic, on_device(): jax.ops.segment_sum(back_rows, slot_position.reshape(-1), num_segments=fe...  87.4 us
    psum x1, waiting for transfers between devices, on_device(): lax.psum(column_sum.astype(jnp.bfloat16), 'label').astype(jnp.float32)  52.6 us
    all_to_all x1, waiting for transfers between devices, on_device(): lax.all_to_all(group_part, 'feat', split_axis=0, concat_axis=0, tiled=True)  44 us
    all_to_all x1, waiting for transfers between devices, on_device(): lax.all_to_all(outgoing, 'feat', split_axis=0, concat_axis=0, tiled=True)  36.4 us
    scatter-add x1, other arithmetic, on_device(): jax.ops.segment_sum(returned.astype(jnp.float32).reshape(feat_count * CAP...  22.5 us
    reduce_sum x1, other arithmetic, on_device(): summed_pre = jnp.sum(lax.all_gather(partial_pre, 'label'), axis=0)  18 us
  transfers between devices with their start and end apart: 4, of which 4 were waited for; matrix products, arithmetic and copies ran while one was open for 4% of the time, Pallas kernels for 0%

profile of v1, /device:TPU:0, one launch (start us, length us, event | category | flops | bytes accessed | tf_op | source)
XLA Modules:
  0.0 763.1 jit_solution(13063993140037701146)
XLA Ops:
  7.2 1.5 copy-done
  8.8 4.0 convolution_bitcast_fusion
  12.8 7.6 while.1
  12.8 0.1 constant_dynamic-slice_fusion.3
  12.9 0.5 slice.26
  13.4 1.3 bitcast_dynamic-update-slice_fusion.2
  14.7 0.1 constant_dynamic-slice_fusion.3
  14.8 0.5 slice.26
  15.3 1.3 bitcast_dynamic-update-slice_fusion.2
  16.6 0.1 constant_dynamic-slice_fusion.3
  16.7 0.5 slice.26
  17.2 1.3 bitcast_dynamic-update-slice_fusion.2
  18.5 0.1 constant_dynamic-slice_fusion.3
  18.6 0.5 slice.26
  19.1 1.3 bitcast_dynamic-update-slice_fusion.2
  20.4 0.1 copy.28
  20.5 0.1 eq.43
  20.6 0.2 compare_reduce_fusion.1
  20.8 0.1 copy.29
  21.0 1.0 sort.17
  22.0 0.1 copy.33
  22.1 0.1 reshape.170
  22.2 0.1 copy.32
  22.3 352.2 %all-gather.3.cloned.1.call-done = f32[512,160,128]{2,1,0:T(8,128)} async-done(((f32[64,160,128]{2,1,0:T(8,128)}), f32[512,160,128]{2,1,0:T(8,128)}) %all-gather.3.cloned.1.call-update) | async-done | bytes 41943056 | tf_op jit(solution)/shard_map/all_gather | solution.py:26
  374.5 18.0 %reduce_sum.9 = bf16[64,160,128]{2,1,0:T(8,128)(2,1)} reduce(f32[8,64,160,128]{3,2,1,0:T(8,128)} %bitcast.63, f32[]{:T(128)} %constant.24.clone.1), dimensions={0}, to_apply=%region_0.0 | reduce | flops 9175040 | bytes 44564484 | tf_op jit(solution)/shard_map/reduce_sum | solution.py:26
  392.5 3.8 maximum_convert_fusion
  396.2 4.8 gather_fusion.1
  401.1 4.5 broadcast_select_fusion.5
  405.5 5.0 all-to-all-start
  410.5 0.8 constant_dynamic-slice_fusion.1
  411.3 0.1 copy.39
  411.4 0.1 eq.47
  411.5 0.1 reshape.162
  411.6 0.1 fusion.16
  411.7 0.1 reshape.157
  411.8 0.2 reduce_window_sum.11
  412.1 0.1 add_add_fusion
  412.1 0.1 add.132
  412.2 2.8 gather_fusion
  415.0 0.1 reshape.161
  415.1 0.1 reshape.186
  415.2 0.1 reshape.178
  415.3 0.1 copy.34
  415.5 3.7 compare_reduce_fusion
  419.2 36.4 %all-to-all-done = bf16[4,24,160,128]{3,2,1,0:T(8,128)(2,1)} async-done(((bf16[4,24,160,128]{3,2,1,0:T(8,128)(2,1)}), bf16[4,24,160,128]{3,2,1,0:T(8,128)(2,1)}, u32[]{:S(2)}, u32[]{:S(2)}) %all-to-all-start) | async-done | bytes 3932192 | tf_op jit(solution)/shard_map/all_to_all | solution.py:41
  455.6 14.7 %gather_fusion.2 = bf16[384,160,128]{2,1,0:T(8,128)(2,1)} fusion(bf16[96,160,128]{2,1,0:T(8,128)(2,1)} %bitcast.4, s32[1024]{0:T(1024)S(1)} %pad_clamp_fusion), kind=kCustom, calls=%fused_computation.2 | custom fusion | bytes 31458816 | tf_op jit(solution)/shard_map/jit(_take)/gather | solution.py:48
  470.4 11.4 %fusion.14 = bf16[160,24,128,1]{2,0,3,1:T(8,128)(2,1)S(1)} fusion(pred[160,24,128]{2,1,0:T(8,128)(4,1)S(1)} %compare_reduce_fusion, bf16[24,16,128,128]{3,2,1,0:T(8,128)(2,1)} %param.7, bf16[24,16,160,128]{3,2,1,0:T(8,128)(2,1)} %bitcast.64, pred[24,16]{1,0:T(8,128)(4,1)S(1)} %get-tuple-element.28), kind=kOutput, calls=%fused_computation.30 | convolution fusion | flops 2024079360 | bytes 29786496 | tf_op jit(solution)/shard_map/lsdc,lsce->dle/dot_general | solution.py:49
  481.8 15.2 %fusion.23 = f32[24,160,16,128]{3,1,2,0:T(8,128)} fusion(bf16[160,24,128,1]{2,0,3,1:T(8,128)(2,1)S(1)} %fusion.14, bf16[24,16,128,128]{3,2,1,0:T(8,128)(2,1)} %param.7), kind=kOutput, calls=%fused_computation.58 | convolution fusion | flops 2013265920 | bytes 45023232 | tf_op jit(solution)/shard_map/dle,lsce->lsdc/dot_general | solution.py:60
  497.0 4.2 broadcast_in_dim.58
  501.2 87.4 %scatter_fusion = f32[96,160,128]{2,1,0:T(8,128)} fusion(f32[96,160,128]{2,1,0:T(8,128)} %broadcast_in_dim.58, s32[384]{0:T(512)S(1)} %reshape.186, f32[384,160,128]{2,1,0:T(8,128)} %bitcast.62), kind=kCustom, calls=%fused_computation.3 | custom fusion | flops 7864320 | bytes 94373376 | tf_op jit(solution)/shard_map/scatter-add | solution.py:62
  588.6 5.8 convert_element_type.45
  594.5 4.8 all-to-all-start.1
  599.3 0.3 all-reduce.3.cloned.1.call-start
  599.6 0.1 copy.30
  599.6 0.1 reshape.194
  599.7 44.0 %all-to-all-done.1 = bf16[4,24,160,128]{3,2,1,0:T(8,128)(2,1)} async-done(((bf16[4,24,160,128]{3,2,1,0:T(8,128)(2,1)}), bf16[4,24,160,128]{3,2,1,0:T(8,128)(2,1)}, u32[]{:S(2)}, u32[]{:S(2)}) %all-to-all-start.1) | async-done | bytes 3932192 | tf_op jit(solution)/shard_map/all_to_all | solution.py:66
  643.8 6.4 bitcast_convert_fusion
  650.2 3.0 broadcast.134
  653.1 22.5 %scatter_fusion.1 = f32[64,160,128]{2,1,0:T(8,128)} fusion(f32[64,160,128]{2,1,0:T(8,128)} %broadcast.134, s32[96]{0:T(128)S(1)} %reshape.194, f32[96,160,128]{2,1,0:T(8,128)} %bitcast_convert_fusion), kind=kCustom, calls=%fused_computation.4 | custom fusion | flops 1966080 | bytes 23593344 | tf_op jit(solution)/shard_map/scatter-add | solution.py:67
  675.6 4.4 convert_element_type.46
  680.1 14.4 %fusion.4 = bf16[24,16,128,128]{3,2,1,0:T(8,128)(2,1)} fusion(bf16[160,24,128,1]{2,0,3,1:T(8,128)(2,1)S(1)} %fusion.14, bf16[24,16,160,128]{3,2,1,0:T(8,128)(2,1)} %bitcast.65, pred[24,16]{1,0:T(8,128)(4,1)S(1)} %get-tuple-element.28), kind=kOutput, calls=%fused_computation.13 | convolution fusion | flops 2027421696 | bytes 29294976 | tf_op jit(solution)/shard_map/lsdc,dle->lsce/dot_general | solution.py:57
  694.4 52.6 %all-reduce.3.cloned.1.call-done = bf16[64,160,128]{2,1,0:T(8,128)(2,1)} async-done(((bf16[64,160,128]{2,1,0:T(8,128)(2,1)}), bf16[64,160,128]{2,1,0:T(8,128)(2,1)}) %all-reduce.3.cloned.1.call-update) | async-done | bytes 2621456 | tf_op jit(solution)/shard_map/psum | solution.py:72
  747.0 5.2 fusion.13
  752.2 4.1 copy.36
  (28 shorter events, 0.3 us)
Async XLA Ops:
  7.2 1.6 copy-start
  7.2 367.3 %all-gather.3.cloned.1.call-start = ((), (), s32[]{:S(2)}) async-start(), calls=%async_computation.3 | async-start | bytes 47185920 | tf_op jit(solution)/shard_map/all_gather | solution.py:26
  405.5 50.1 %all-to-all-start = ((bf16[4,24,160,128]{3,2,1,0:T(8,128)(2,1)}), bf16[4,24,160,128]{3,2,1,0:T(8,128)(2,1)}, u32[]{:S(2)}, u32[]{:S(2)}) async-start(bf16[4,24,160,128]{3,2,1,0:T(8,128)(2,1)} %broadcast_select_fusion.5), calls=%async_computation | async-start | bytes 7864320 | tf_op jit(solution)/shard_map/all_to_all | solution.py:41
  412.2 3.1 copy-start.3
  594.5 49.3 %all-to-all-start.1 = ((bf16[4,24,160,128]{3,2,1,0:T(8,128)(2,1)}), bf16[4,24,160,128]{3,2,1,0:T(8,128)(2,1)}, u32[]{:S(2)}, u32[]{:S(2)}) async-start(bf16[4,24,160,128]{3,2,1,0:T(8,128)(2,1)} %bitcast.66), calls=%async_computation.1 | async-start | bytes 7864320 | tf_op jit(solution)/shard_map/all_to_all | solution.py:66
  599.3 147.7 %all-reduce.3.cloned.1.call-start = ((), (), s32[]{:S(2)}) async-start(), calls=%async_computation.2 | async-start | bytes 5242880 | tf_op jit(solution)/shard_map/psum | solution.py:72
  680.0 67.0 %copy-start.2 = (bf16[160,128]{1,0:T(8,128)(2,1)S(1)}, bf16[160,128]{1,0:T(8,128)(2,1)}, u32[]{:S(2)}) copy-start(bf16[160,128]{1,0:T(8,128)(2,1)} %param.5) | copy-start | bytes 122884
  680.0 76.2 %copy-start.1 = (bf16[128,8192]{1,0:T(8,128)(2,1)S(1)}, bf16[128,8192]{1,0:T(8,128)(2,1)}, u32[]{:S(2)}) copy-start(bf16[128,8192]{1,0:T(8,128)(2,1)} %param.6) | copy-start | bytes 6291460
Sparse Core Ops, SparseCore 0:
  12.9 361.5 all-gather.2
  680.2 66.8 all-reduce.2
